TPU v7x, 128 devices: a whole 4x4x4 slice. The times are simulated.
128 devices in a mesh: lon: 16 (over y, x), lat: 8 (over z, core).
Axes of the slice: x: 4, y: 4, z: 4, core: 2. Of those that a mesh axis runs over, the one named last changes fastest.
Arguments:
- concentration: float32 [72, 8, 128, 2048], P(None, None, 'lat', 'lon'), may hold values from -0.3 to 0.3
- adjoint: float32 [72, 8, 128, 2048], P(None, None, 'lat', 'lon'), may hold values from -4 to 4
- wind_east: float32 [72, 128, 2048], P(None, 'lat', 'lon'), may hold values from -0.45 to 0.45
- wind_north: float32 [72, 128, 2048], P(None, 'lat', 'lon'), may hold values from -0.45 to 0.45
- mixing: float32 [72, 128, 2048], P(None, 'lat', 'lon'), may hold values from 0.01 to 100
- sound_col: int32 [1, 128, 4096], P(None, ('lon', 'lat')), may hold values from -1 to 2047, as said below
- kernel: float32 [72, 128, 4096], P(None, ('lon', 'lat')), may hold values from 0.5 to 3
- observed: float32 [1, 128, 4096], P(None, ('lon', 'lat')), may hold values from -12 to 12
- obs_error: float32 [1, 128, 4096], P(None, ('lon', 'lat')), may hold values from 1 to 3
Outputs:
- adjoint_out: float32 [72, 8, 128, 2048], P(None, None, 'lat', 'lon')
- residual: float32 [1, 128, 4096], P(None, ('lon', 'lat'))
Inputs may be any that keep to these rules, and one draw needn't show every extreme that they name: `sound_col`: each entry is a column index inside the brick of its slot (slots b * 32 to b * 32 + 31 of an owner belong to brick b in lon-major order), or -1 for an empty slot; for each owner and brick the used slots come first. In every draw some brick receives 32 soundings from every owner.
All inputs are finite; a program needn't handle non-finite values.
Results may differ from a plain program's by a relative error of at most 0.00022.
Values sent between devices are 32-bit elements; how exact they have to be, the bound alone decides.
A program may use at most 192 MiB of HBM per device.

v0:
```python
import functools

import jax
import jax.numpy as jnp
from jax import lax
from jax.experimental import pallas as pl
from jax.experimental.pallas import tpu as pltpu
from jax.sharding import PartitionSpec as P

MESH = pl.DeviceIdType.MESH
LANES = 128
ROWS = 16
TRACERS = 8
BLOCK = TRACERS * ROWS
F32 = jnp.float32
BF16 = jnp.bfloat16


def lane_ids(rows):
    return lax.broadcasted_iota(jnp.int32, (rows, LANES), 1)


def row_ids(rows):
    return lax.broadcasted_iota(jnp.int32, (rows, LANES), 0)


def swap_blocks(v, lane):
    low = lane < 64
    even = (lane // 32) % 2 == 0
    out = []
    first = [None] * 4
    for b in range(2):
        first[b] = jnp.where(low, v[b], pltpu.roll(v[2 + b], 64, 1))
        first[2 + b] = jnp.where(low, pltpu.roll(v[b], 64, 1), v[2 + b])
    for h in range(2):
        a, b = first[2 * h], first[2 * h + 1]
        out.append(jnp.where(even, a, pltpu.roll(b, 32, 1)))
        out.append(jnp.where(even, pltpu.roll(a, 96, 1), b))
    return out


def pack_lon(src, blocks, dst):
    lane = lane_ids(8)
    pair = ((lane + 127) % 128) // 2

    def group(g, count):
        acc = jnp.zeros((8, LANES), F32)
        for kk in range(count):
            for j in range(16):
                slot = kk * 16 + j
                v = src[pl.ds(pl.multiple_of((g * 4 + kk) * BLOCK + j * 8, 8), 8), :]
                acc = jnp.where(pair == slot, pltpu.roll(v, (2 * slot + 2) % LANES, 1), acc)
        dst[pl.ds(pl.multiple_of(g * 8, 8), 8), :] = acc

    def body(g, c):
        group(g, 4)
        return c

    lax.fori_loop(0, blocks // 4, body, 0)
    if blocks % 4:
        group(blocks // 4, blocks % 4)


def pack_lat(src, blocks, row, dst):
    def body(k, c):
        dst[pl.ds(pl.multiple_of(k * 8, 8), 8), :] = src[pl.ds(k * BLOCK + row, 8, stride=ROWS), :]
        return c

    lax.fori_loop(0, blocks, body, 0, unroll=3)


def merge_lon(west, east, groups, dst):
    odd = lane_ids(8) % 2 == 1

    def body(g, c):
        rows = pl.ds(pl.multiple_of(g * 8, 8), 8)
        dst[rows, :] = jnp.where(odd, west[rows, :], pltpu.roll(east[rows, :], 126, 1))
        return c

    lax.fori_loop(0, groups, body, 0)


def outer_columns(merged, block, j):
    rows = pl.ds(pl.multiple_of((block // 4) * 8, 8), 8)
    v = merged[rows, :]
    slot = lax.rem(block, 4) * 16 + 2 * j
    return jnp.concatenate(
        [pltpu.roll(v, LANES - 1 - 2 * slot, 1), pltpu.roll(v, LANES - 3 - 2 * slot, 1)], axis=0
    )


def transport(field, levels, tracers, merged, south, north, coef):
    lane = lane_ids(ROWS)
    row = row_ids(ROWS)
    first_lane, last_lane = lane == 0, lane == LANES - 1
    first_row, last_row = row == 0, row == ROWS - 1
    c0, ce, cw, cn, cs, ca, cg = coef

    def down(block, j, level, above):
        at = pl.multiple_of(block * BLOCK + j * ROWS, 8)
        v = field[pl.ds(at, ROWS), :]
        cols = outer_columns(merged, block, j)
        edge = block * 8 + j
        lo = jnp.broadcast_to(south[pl.ds(edge, 1), :], (ROWS, LANES))
        hi = jnp.broadcast_to(north[pl.ds(edge, 1), :], (ROWS, LANES))
        east = jnp.where(last_lane, cols, pltpu.roll(v, LANES - 1, 1))
        west = jnp.where(first_lane, cols, pltpu.roll(v, 1, 1))
        up = jnp.where(last_row, hi, pltpu.roll(v, ROWS - 1, 0))
        dn = jnp.where(first_row, lo, pltpu.roll(v, 1, 0))
        new = level[0] * v + level[1] * east + level[2] * west + level[3] * up + level[4] * dn + level[5] * above
        field[pl.ds(at, ROWS), :] = new
        return new

    def at_level(k, refs):
        rows = pl.ds(pl.multiple_of(k * ROWS, ROWS), ROWS)
        return [ref[rows, :] for ref in refs]

    if tracers == TRACERS:

        def down_body(k, carry):
            level = at_level(k, (c0, ce, cw, cn, cs, ca))
            return tuple(down(k, t, level, carry[t]) for t in range(TRACERS))

        zero = jnp.zeros((ROWS, LANES), F32)
        last = lax.fori_loop(0, levels, down_body, (zero,) * TRACERS)

        def up_body(i, carry):
            k = levels - 2 - i
            g = at_level(k, (cg,))[0]
            out = []
            for t in range(TRACERS):
                rows = pl.ds(pl.multiple_of(k * BLOCK + t * ROWS, 8), ROWS)
                new = field[rows, :] + g * carry[t]
                field[rows, :] = new
                out.append(new)
            return tuple(out)

        lax.fori_loop(0, levels - 1, up_body, last)
    else:

        def down_one(a, carry):
            for b in range(8):
                carry = down(a, b, at_level(a * 8 + b, (c0, ce, cw, cn, cs, ca)), carry)
            return carry

        last = lax.fori_loop(0, levels // 8, down_one, jnp.zeros((ROWS, LANES), F32))

        def up_one(i, carry):
            for b in range(8):
                k = levels - 1 - (i * 8 + b)
                rows = pl.ds(pl.multiple_of(k * ROWS, ROWS), ROWS)
                carry = field[rows, :] + cg[rows, :] * carry
                field[rows, :] = carry
            return carry

        lax.fori_loop(0, levels // 8, up_one, jnp.zeros((ROWS, LANES), F32))


def window_kernel(
    n_lon, n_lat, levels,
    conc_hbm, adj_hbm, we_hbm, wn_hbm, mix_hbm, col_hbm, kern_hbm, obs_hbm, err_hbm,
    adj_out, force_out, res_out,
    field, conc, we, wn, mix, prof, force, c0, ce, cw, cn, cs, ca, cg,
    kv, colv, obsv, errv, sendb, recvb, kn, coln, wres, resb,
    lhs, rhs,
    q_adj0, q_adj1, q_one, lat_a, lat_b, lat_one_a, lat_one_b,
    w_adj0, e_adj0, w_adj1, e_adj1, s_adj0, n_adj0, s_adj1, n_adj1,
    w_one, e_one, s_one, n_one, m_adj, m_one,
    load_sem, out_sem, a2a_send, a2a_recv, res_send, res_recv, self_sem, halo_send, halo_recv, stage_sem,
):
    lon, lat = lax.axis_index("lon"), lax.axis_index("lat")
    bricks = n_lon * n_lat
    me = lon * n_lat + lat
    per = levels // 4 + 1
    tiles = bricks // 4
    groups = tiles // 8

    loads = [
        (kern_hbm, kv), (col_hbm, colv), (obs_hbm, obsv), (err_hbm, errv), (we_hbm, we), (wn_hbm, wn),
        (adj_hbm, field), (mix_hbm, mix), (conc_hbm, conc),
    ]
    loads = [pltpu.make_async_copy(a, b, load_sem.at[i]) for i, (a, b) in enumerate(loads)]
    for copy in loads:
        copy.start()

    barrier = pltpu.get_barrier_semaphore()
    for d in range(1, n_lat):
        pl.semaphore_signal(barrier, inc=1, device_id=(lon, lax.rem(lat + d, n_lat)), device_id_type=MESH)
    for d in range(1, n_lon):
        pl.semaphore_signal(barrier, inc=1, device_id=(lax.rem(lon + d, n_lon), lat), device_id_type=MESH)

    lane8 = lane_ids(8)
    for i in range(4):
        loads[i].wait()

    def pack_rows(kk, c, v):
        y = swap_blocks(v, lane8)
        for m in range(4):
            sendb[pl.ds((c * 32 + m) * per + kk, 8, stride=4 * per), :] = y[m]

    def pack_body(kk, carry):
        for c in range(groups):
            pack_rows(kk, c, [kv[pl.ds(pl.multiple_of((kk * 4 + q) * tiles + c * 8, 8), 8), :] for q in range(4)])
        return carry

    lax.fori_loop(0, levels // 4, pack_body, 0)
    for c in range(groups):
        rows = pl.ds(c * 8, 8)
        e = errv[rows, :]
        pack_rows(levels // 4, c, [colv[rows, :].astype(F32), obsv[rows, :], e, e])

    loads[4].wait()
    loads[5].wait()
    pack_lon(we, levels // 8, q_one.at[0])
    pack_lat(wn, levels // 8, ROWS - 1, lat_one_a.at[0])
    loads[6].wait()
    pack_lon(field, levels, q_adj0)
    pack_lat(field, levels, ROWS - 1, lat_a.at[0])
    pack_lat(field, levels, 0, lat_b.at[0])

    pl.semaphore_wait(barrier, n_lon + n_lat - 2)
    for d in range(1, n_lat):
        pl.semaphore_signal(stage_sem, inc=1, device_id=(lon, lax.rem(lat + d, n_lat)), device_id_type=MESH)
    pl.semaphore_wait(stage_sem, n_lat - 1)

    east = (lax.rem(lon + 1, n_lon), lat)
    west = (lax.rem(lon + n_lon - 1, n_lon), lat)
    north = (lon, lax.rem(lat + 1, n_lat))
    south = (lon, lax.rem(lat + n_lat - 1, n_lat))

    def remote(src, dst, index, device):
        return pltpu.make_async_remote_copy(
            src, dst, halo_send.at[index], halo_recv.at[index], device_id=device, device_id_type=MESH
        )

    def exchange(first, q, top, bottom, w, e, s, n):
        copies = [
            remote(top, s, first, north), remote(bottom, n, first + 1, south),
            remote(q, w, first + 2, east), remote(q, e, first + 3, west),
        ]
        for copy in copies:
            copy.start()
        return copies

    def land(copies):
        for copy in copies:
            copy.wait()

    wind_copies = [
        remote(q_one.at[0], w_one.at[0], 0, east), remote(lat_one_a.at[0], s_one.at[0], 1, north),
    ]
    for copy in wind_copies:
        copy.start()
    halo = exchange(2, q_adj0, lat_a.at[0], lat_b.at[0], w_adj0, e_adj0, s_adj0, n_adj0)

    def peer(i):
        d = lax.rem(i * 37, bricks)
        tl, ta = lax.rem(lon + d // n_lat, n_lon), lax.rem(lat + lax.rem(d, n_lat), n_lat)
        return tl, ta, tl * n_lat + ta

    def send_body(i, c):
        tl, ta, t = peer(i)
        pltpu.make_async_remote_copy(
            sendb.at[pl.ds(t * per, per)], recvb.at[pl.ds(me * per, per)], a2a_send, a2a_recv,
            device_id=(tl, ta), device_id_type=MESH,
        ).start()
        return c

    lax.fori_loop(1, bricks, send_body, 0)
    own = pltpu.make_async_copy(sendb.at[pl.ds(me * per, per)], recvb.at[pl.ds(me * per, per)], self_sem)
    own.start()

    loads[7].wait()
    loads[8].wait()

    def tracer_sum(k, c):
        total = conc[pl.ds(pl.multiple_of(k * BLOCK, 8), ROWS), :]
        for t in range(1, TRACERS):
            total = total + conc[pl.ds(pl.multiple_of(k * BLOCK + t * ROWS, 8), ROWS), :]
        prof[pl.ds(pl.multiple_of(k * ROWS, 8), ROWS), :] = total
        return c

    lax.fori_loop(0, levels, tracer_sum, 0, unroll=2)

    land(wind_copies)
    lane = lane_ids(ROWS)
    row = row_ids(ROWS)
    merge_lon(w_one.at[0], w_one.at[0], (levels // 8 + 3) // 4, m_one)
    southmost = lat == 0
    northmost = lat == n_lat - 1
    open_north = jnp.logical_not(jnp.logical_and(row == ROWS - 1, northmost)).astype(F32)
    open_south = jnp.where(southmost, 0.0, 1.0)

    def coefficients(a, carry):
        above, factor = carry
        for b in range(8):
            k = a * 8 + b
            rows = pl.ds(pl.multiple_of(k * ROWS, ROWS), ROWS)
            u, n = we[rows, :], wn[rows, :]
            cols = outer_columns(m_one, a, b)
            u_west = jnp.where(lane == 0, cols, pltpu.roll(u, 1, 1))
            edge = jnp.broadcast_to(s_one[0, pl.ds(k, 1), :], (ROWS, LANES)) * open_south
            n_south = jnp.where(row == 0, edge, pltpu.roll(n, 1, 0))
            ep, wm = jnp.maximum(u, 0.0), jnp.minimum(u_west, 0.0)
            up, sm = jnp.maximum(n, 0.0), jnp.minimum(n_south, 0.0)
            below = mix[rows, :] * jnp.where(k < levels - 1, 1.0, 0.0)
            inv = 1.0 / (1.0 + below + above - above * factor)
            c0[rows, :] = (1.0 - ep + wm - up + sm) * inv
            ce[rows, :] = ep * inv
            cw[rows, :] = -wm * inv
            cn[rows, :] = up * open_north * inv
            cs[rows, :] = -sm * inv
            ca[rows, :] = above * inv
            factor = below * inv
            cg[rows, :] = factor
            above = below
        return above, factor

    zero = jnp.zeros((ROWS, LANES), F32)
    lax.fori_loop(0, levels // 8, coefficients, (zero, zero))
    coef = (c0, ce, cw, cn, cs, ca, cg)

    land(halo)
    merge_lon(w_adj0, e_adj0, levels // 4, m_adj)
    transport(field, levels, TRACERS, m_adj, s_adj0, n_adj0, coef)
    pack_lon(field, levels, q_adj1)
    pack_lat(field, levels, ROWS - 1, lat_a.at[1])
    pack_lat(field, levels, 0, lat_b.at[1])
    halo = exchange(6, q_adj1, lat_a.at[1], lat_b.at[1], w_adj1, e_adj1, s_adj1, n_adj1)
    land(halo)
    merge_lon(w_adj1, e_adj1, levels // 4, m_adj)
    transport(field, levels, TRACERS, m_adj, s_adj1, n_adj1, coef)
    adj_copy = pltpu.make_async_copy(field, adj_out, out_sem.at[0])
    adj_copy.start()

    own.wait()
    rest = pl.ds(0, (bricks - 1) * per)
    pltpu.make_async_copy(recvb.at[rest], recvb.at[rest], a2a_recv).wait()

    def unpack(kk, c):
        z = [recvb[pl.ds((c * 32 + m) * per + kk, 8, stride=4 * per), :] for m in range(4)]
        return swap_blocks(z, lane8)

    def unpack_body(kk, carry):
        for c in range(groups):
            v = unpack(kk, c)
            for q in range(4):
                kn[pl.ds(pl.multiple_of((kk * 4 + q) * tiles + c * 8, 8), 8), :] = v[q]
        return carry

    lax.fori_loop(0, levels // 4, unpack_body, 0)
    aux = [unpack(levels // 4, c) for c in range(groups)]
    cols = [aux[c][0].astype(jnp.int32) for c in range(groups)]
    spots = [lax.bitwise_and(v, LANES - 1) for v in cols]
    bits = [[lax.bitwise_and(v, LANES << b) != 0 for b in range(4)] for v in cols]

    def gather_body(k, acc):
        rows = [
            jnp.broadcast_to(prof[pl.ds(k * ROWS + r, 1), :], (8, LANES)) for r in range(ROWS)
        ]
        out = []
        for c in range(groups):
            picked = [jnp.take_along_axis(v, spots[c], axis=1, mode="promise_in_bounds") for v in rows]
            for b in range(4):
                picked = [jnp.where(bits[c][b], picked[2 * i + 1], picked[2 * i]) for i in range(len(picked) // 2)]
            out.append(acc[c] + kn[pl.ds(pl.multiple_of(k * tiles + c * 8, 8), 8), :] * picked[0])
        return tuple(out)

    modelled = lax.fori_loop(0, levels, gather_body, (jnp.zeros((8, LANES), F32),) * groups)
    for c in range(groups):
        rows = pl.ds(c * 8, 8)
        res = jnp.where(cols[c] >= 0, (modelled[c] - aux[c][1]) / aux[c][2], 0.0)
        wres[rows, :] = res
        coln[rows, :] = cols[c]
        obsv[rows, :] = res / aux[c][2]

    def res_body(i, c):
        tl, ta, t = peer(i)
        pltpu.make_async_remote_copy(
            wres.at[pl.ds(t // 4, 1)], resb.at[pl.ds(me, 1)], res_send, res_recv,
            device_id=(tl, ta), device_id_type=MESH,
        ).start()
        return c

    lax.fori_loop(1, bricks, res_body, 0)
    own_res = pltpu.make_async_copy(wres.at[pl.ds(me // 4, 1)], resb.at[pl.ds(me, 1)], self_sem)
    own_res.start()

    def weigh(k, c):
        for g in range(groups):
            rows = pl.ds(pl.multiple_of(k * tiles + g * 8, 8), 8)
            kn[rows, :] = kn[rows, :] * obsv[pl.ds(g * 8, 8), :]
        return c

    lax.fori_loop(0, levels, weigh, 0)

    cell = lax.broadcasted_iota(jnp.int32, (2 * LANES, LANES), 0)

    def build(c, carry):
        lanes = pl.ds(pl.multiple_of(c * LANES, LANES), LANES)
        w = kn[pl.ds(c, levels, stride=tiles), :]
        high = w.astype(BF16)
        low = (w - high.astype(F32)).astype(BF16)
        lhs[pl.ds(0, levels), lanes] = high
        lhs[pl.ds(levels, levels), lanes] = low
        col = jnp.broadcast_to(coln[pl.ds(c, 1), :], (2 * LANES, LANES))
        rhs[:, lanes] = jnp.where(lax.bitwise_and(col, 2 * LANES - 1) == cell, 1.0, 0.0).astype(BF16)
        return carry

    lax.fori_loop(0, tiles, build, 0)
    colrow = jnp.concatenate([coln[pl.ds(c, 1), :] for c in range(tiles)], axis=1)

    def scatter(r, carry):
        mine = jnp.where(lax.shift_right_arithmetic(colrow, 8) == r, 1.0, 0.0).astype(BF16)
        out = lax.dot_general(
            lhs[...] * mine, rhs[...], (((1,), (1,)), ((), ())), preferred_element_type=F32
        )
        both = out[:levels] + out[levels:]
        force[pl.ds(2 * r, levels, stride=ROWS), :] = both[:, :LANES]
        force[pl.ds(2 * r + 1, levels, stride=ROWS), :] = both[:, LANES:]
        return carry

    lax.fori_loop(0, ROWS // 2, scatter, 0)

    for step in (1, 2):
        pack_lon(force, levels // 8, q_one.at[step])
        pack_lat(force, levels // 8, ROWS - 1, lat_one_a.at[step])
        pack_lat(force, levels // 8, 0, lat_one_b.at[step])
        halo = exchange(
            6 + 4 * step, q_one.at[step], lat_one_a.at[step], lat_one_b.at[step],
            w_one.at[step], e_one.at[step], s_one.at[step], n_one.at[step],
        )
        land(halo)
        merge_lon(w_one.at[step], e_one.at[step], (levels // 8 + 3) // 4, m_one)
        transport(force, levels, 1, m_one, s_one.at[step], n_one.at[step], coef)
    force_copy = pltpu.make_async_copy(force, force_out, out_sem.at[1])
    force_copy.start()

    own_res.wait()
    rest_res = pl.ds(0, bricks - 1)
    pltpu.make_async_copy(resb.at[rest_res], resb.at[rest_res], res_recv).wait()
    mine_block = lax.rem(me, 4)
    for g in range(groups):
        total = jnp.zeros((8, LANES), F32)
        for m in range(4):
            v = resb[pl.ds(g * 32 + m, 8, stride=4), :]
            shift = lax.rem((m - mine_block + 4) * 32, LANES)
            total = jnp.where(lane8 // 32 == m, pltpu.roll(v, shift, 1), total)
        errv[pl.ds(g * 8, 8), :] = total
    res_copy = pltpu.make_async_copy(errv, res_out, out_sem.at[2])
    res_copy.start()

    pltpu.make_async_copy(recvb.at[rest], recvb.at[rest], a2a_send).wait()
    pltpu.make_async_copy(resb.at[rest_res], resb.at[rest_res], res_send).wait()
    adj_copy.wait()
    force_copy.wait()
    res_copy.wait()


def add_kernel(field, force, res, out, res_out):
    for k in range(8):
        one = force[k * ROWS : (k + 1) * ROWS, :]
        for t in range(TRACERS):
            rows = pl.ds(k * BLOCK + t * ROWS, ROWS)
            out[rows, :] = field[rows, :] + one
    res_out[...] = res[...]


def per_device(n_lon, n_lat, concentration, adjoint, wind_east, wind_north, mixing, sound_col, kernel, observed, obs_error):
    levels, tracers, row_count, col_count = adjoint.shape
    bricks = n_lon * n_lat
    slots = sound_col.shape[2]
    tiles = slots // LANES
    per = levels // 4 + 1
    big, one = (levels * BLOCK, LANES), (levels * ROWS, LANES)
    q_rows, q_one_rows = levels // 4 * 8, (levels // 8 + 3) // 4 * 8
    hbm = pl.BlockSpec(memory_space=pl.ANY)
    vm = lambda *shape: pltpu.VMEM(shape, F32)
    scratch = (
        [vm(*big), vm(*big)] + [vm(*one)] * 12
        + [vm(levels * tiles, LANES), pltpu.VMEM((tiles, LANES), jnp.int32), vm(tiles, LANES), vm(tiles, LANES)]
        + [vm(bricks * per, LANES), vm(bricks * per, LANES), vm(levels * tiles, LANES)]
        + [pltpu.VMEM((tiles, LANES), jnp.int32), vm(tiles, LANES), vm(bricks, LANES)]
        + [pltpu.VMEM((2 * levels, slots), BF16), pltpu.VMEM((2 * LANES, slots), BF16)]
        + [vm(q_rows, LANES), vm(q_rows, LANES), vm(3, q_one_rows, LANES)]
        + [vm(2, levels * 8, LANES), vm(2, levels * 8, LANES), vm(3, levels, LANES), vm(3, levels, LANES)]
        + [vm(q_rows, LANES)] * 4 + [vm(levels * 8, LANES)] * 4
        + [vm(3, q_one_rows, LANES), vm(3, q_one_rows, LANES), vm(3, levels, LANES), vm(3, levels, LANES)]
        + [vm(q_rows, LANES), vm(q_one_rows, LANES)]
        + [pltpu.SemaphoreType.DMA((9,)), pltpu.SemaphoreType.DMA((3,))]
        + [pltpu.SemaphoreType.DMA] * 5
        + [pltpu.SemaphoreType.DMA((18,)), pltpu.SemaphoreType.DMA((18,)), pltpu.SemaphoreType.REGULAR]
    )
    field, force, res = pl.pallas_call(
        functools.partial(window_kernel, n_lon, n_lat, levels),
        out_shape=(
            jax.ShapeDtypeStruct(big, F32), jax.ShapeDtypeStruct(one, F32), jax.ShapeDtypeStruct((tiles, LANES), F32),
        ),
        in_specs=[hbm] * 9,
        out_specs=(hbm,) * 3,
        scratch_shapes=scratch,
        compiler_params=pltpu.CompilerParams(collective_id=0, has_side_effects=True, vmem_limit_bytes=48 << 20),
        name="window",
    )(
        concentration.reshape(big), adjoint.reshape(big), wind_east.reshape(one), wind_north.reshape(one),
        mixing.reshape(one), sound_col.reshape(tiles, LANES), kernel.reshape(levels * tiles, LANES),
        observed.reshape(tiles, LANES), obs_error.reshape(tiles, LANES),
    )
    out, residual = pl.pallas_call(
        add_kernel,
        grid=(levels // 8,),
        out_shape=(jax.ShapeDtypeStruct(big, F32), jax.ShapeDtypeStruct((tiles, LANES), F32)),
        in_specs=[
            pl.BlockSpec((8 * BLOCK, LANES), lambda i: (i, 0)),
            pl.BlockSpec((8 * ROWS, LANES), lambda i: (i, 0)),
            pl.BlockSpec((tiles, LANES), lambda i: (0, 0)),
        ],
        out_specs=(pl.BlockSpec((8 * BLOCK, LANES), lambda i: (i, 0)), pl.BlockSpec((tiles, LANES), lambda i: (0, 0))),
        name="combine",
    )(field, force, res)
    return out.reshape(adjoint.shape), residual.reshape(observed.shape)


def solution(mesh):
    in_specs = (
        P(None, None, "lat", "lon"),
        P(None, None, "lat", "lon"),
        P(None, "lat", "lon"),
        P(None, "lat", "lon"),
        P(None, "lat", "lon"),
        P(None, ("lon", "lat"), None),
        P(None, ("lon", "lat"), None),
        P(None, ("lon", "lat"), None),
        P(None, ("lon", "lat"), None),
    )
    out_specs = (P(None, None, "lat", "lon"), P(None, ("lon", "lat"), None))
    return jax.shard_map(
        functools.partial(per_device, mesh.shape["lon"], mesh.shape["lat"]),
        mesh=mesh, in_specs=in_specs, out_specs=out_specs, check_vma=False,
    )
```

profile of v0, /device:TPU:1, one launch (start us, length us, event | category | flops | bytes accessed | tf_op | source)
XLA Modules:
  0.0 117.7 jit_solution(9914008092468634436)
XLA Ops:
  0.6 0.0 copy-start
  0.6 1.3 %copy-done = f32[72,1,4096]{2,1,0:T(1,128)S(1)} copy-done((f32[72,1,4096]{2,1,0:T(1,128)S(1)}, f32[72,1,4096]{2,1,0:T(1,128)}, u32[]{:S(2)}) %copy-start) | copy-done | bytes 1179672
  1.9 0.0 copy-start.1
  1.9 1.1 copy-done.1
  3.0 0.0 copy-start.2
  3.0 1.1 copy-done.2
  4.0 0.0 copy-start.3
  4.0 1.1 copy-done.3
  5.1 0.0 copy-start.5
  5.1 0.7 copy-done.5
  5.8 0.0 copy-start.6
  5.8 0.7 copy-done.6
  6.5 0.0 copy-start.7
  6.5 0.7 copy-done.7
  7.3 101.6 %window.1 = (f32[9216,128]{1,0:T(8,128)}, f32[1152,128]{1,0:T(8,128)S(1)}, f32[32,128]{1,0:T(8,128)S(1)}) custom-call(f32[9216,128]{1,0:T(8,128)} %bitcast.18, f32[9216,128]{1,0:T(8,128)} %bitcast.19, f32[1152,128]{1,0:T(8,128)S(1)} %bitcast.12, f32[1152,128]{1,0:T(8,128)S(1)} %bitcast.13, f32[1152,128]{1,0:T(8,128)S(1)} %bitcast.14, ...), custom_call_target="tpu_custom_call" | custom-call | tf_op jit(solution)/shard_map/window/pallas_call | solution.py:494
  108.9 0.0 copy-start.4
  108.9 0.8 copy-done.4
  109.7 0.0 copy-start.8
  109.7 0.6 copy-done.8
  110.3 7.4 %combine.1 = (f32[9216,128]{1,0:T(8,128)}, f32[32,128]{1,0:T(8,128)}) custom-call(f32[9216,128]{1,0:T(8,128)} %get-tuple-element.7.field, f32[1152,128]{1,0:T(8,128)} %copy-done.4, f32[32,128]{1,0:T(8,128)} %copy-done.8), custom_call_target="tpu_custom_call" | custom-call | tf_op jit(solution)/shard_map/combine/pallas_call | solution.py:509
Async XLA Ops:
  0.6 1.3 %copy-start = (f32[72,1,4096]{2,1,0:T(1,128)S(1)}, f32[72,1,4096]{2,1,0:T(1,128)}, u32[]{:S(2)}) copy-start(f32[72,1,4096]{2,1,0:T(1,128)} %param.15) | copy-start | bytes 3538948
  1.9 1.1 copy-start.1
  3.0 1.1 copy-start.2
  4.0 1.1 copy-start.3
  5.1 0.7 copy-start.5
  5.8 0.7 copy-start.6
  6.5 0.7 copy-start.7
  108.9 0.8 copy-start.4
  109.7 0.6 copy-start.8
where the time goes:
time: 119 us; the launch traced here: 118 us
  Pallas kernels  109 us (92%)
  local copies, waits for them, and re-layouts  8.02 us (7%)
    pallas_call x1, Pallas kernels, per_device(): pl.pallas_call(functools.partial(window_kernel, n_lon, n_lat, levels), ou...  102 us
    unnamed x18, local copies, waits for them, and re-layouts  8.02 us
    pallas_call x1, Pallas kernels, per_device(): pl.pallas_call(add_kernel, grid=(levels // 8,), out_shape=(jax.ShapeDtype...  7.4 us

commit v1 on v0

--- a/solution.py
+++ b/solution.py
@@ -12,6 +12,8 @@
 ROWS = 16
 TRACERS = 8
 BLOCK = TRACERS * ROWS
+COMBINE = 8
+UNROLL = 8
 F32 = jnp.float32
 BF16 = jnp.bfloat16
 
@@ -40,17 +42,25 @@
 
 
 def pack_lon(src, blocks, dst):
-    lane = lane_ids(8)
-    pair = ((lane + 127) % 128) // 2
+    pair = ((lane_ids(8) + 127) % 128) // 2
+    bits = [lax.bitwise_and(pair, 1 << b) != 0 for b in range(6)]
+
+    def tree(parts, level):
+        while len(parts) > 1:
+            parts = [jnp.where(bits[level], parts[2 * i + 1], parts[2 * i]) for i in range(len(parts) // 2)]
+            level += 1
+        return parts[0]
 
     def group(g, count):
-        acc = jnp.zeros((8, LANES), F32)
+        blocks_out = []
         for kk in range(count):
+            parts = []
             for j in range(16):
-                slot = kk * 16 + j
                 v = src[pl.ds(pl.multiple_of((g * 4 + kk) * BLOCK + j * 8, 8), 8), :]
-                acc = jnp.where(pair == slot, pltpu.roll(v, (2 * slot + 2) % LANES, 1), acc)
-        dst[pl.ds(pl.multiple_of(g * 8, 8), 8), :] = acc
+                parts.append(pltpu.roll(v, (2 * (kk * 16 + j) + 2) % LANES, 1))
+            blocks_out.append(tree(parts, 0))
+        blocks_out = (blocks_out * 4)[:4] if count < 4 else blocks_out
+        dst[pl.ds(pl.multiple_of(g * 8, 8), 8), :] = tree(blocks_out, 4)
 
     def body(g, c):
         group(g, 4)
@@ -89,53 +99,79 @@
     )
 
 
-def transport(field, levels, tracers, merged, south, north, coef):
+def transport(field, levels, which, merged, south, north, coef):
     lane = lane_ids(ROWS)
     row = row_ids(ROWS)
     first_lane, last_lane = lane == 0, lane == LANES - 1
     first_row, last_row = row == 0, row == ROWS - 1
     c0, ce, cw, cn, cs, ca, cg = coef
 
-    def down(block, j, level, above):
+    def stencil(block, j, level, above, v, east, west):
         at = pl.multiple_of(block * BLOCK + j * ROWS, 8)
-        v = field[pl.ds(at, ROWS), :]
         cols = outer_columns(merged, block, j)
         edge = block * 8 + j
         lo = jnp.broadcast_to(south[pl.ds(edge, 1), :], (ROWS, LANES))
         hi = jnp.broadcast_to(north[pl.ds(edge, 1), :], (ROWS, LANES))
-        east = jnp.where(last_lane, cols, pltpu.roll(v, LANES - 1, 1))
-        west = jnp.where(first_lane, cols, pltpu.roll(v, 1, 1))
+        east = jnp.where(last_lane, cols, east)
+        west = jnp.where(first_lane, cols, west)
         up = jnp.where(last_row, hi, pltpu.roll(v, ROWS - 1, 0))
         dn = jnp.where(first_row, lo, pltpu.roll(v, 1, 0))
         new = level[0] * v + level[1] * east + level[2] * west + level[3] * up + level[4] * dn + level[5] * above
         field[pl.ds(at, ROWS), :] = new
         return new
 
+    def down(block, j, level, above):
+        v = field[pl.ds(pl.multiple_of(block * BLOCK + j * ROWS, 8), ROWS), :]
+        return stencil(block, j, level, above, v, pltpu.roll(v, LANES - 1, 1), pltpu.roll(v, 1, 1))
+
     def at_level(k, refs):
         rows = pl.ds(pl.multiple_of(k * ROWS, ROWS), ROWS)
         return [ref[rows, :] for ref in refs]
 
-    if tracers == TRACERS:
-
-        def down_body(k, carry):
-            level = at_level(k, (c0, ce, cw, cn, cs, ca))
-            return tuple(down(k, t, level, carry[t]) for t in range(TRACERS))
+    if which is not None:
+
+        count = len(which)
+        source = lax.broadcasted_iota(jnp.int32, (2 * LANES, 2 * LANES), 0) % LANES
+        target = lax.broadcasted_iota(jnp.int32, (2 * LANES, 2 * LANES), 1)
+        shift = jnp.where(target < LANES, target + 1, target - LANES - 1)
+        shift = jnp.where(source == shift, 1.0, 0.0).astype(BF16)
+
+        def down_body(i, carry):
+            values, sides = [], []
+            for u in range(UNROLL):
+                k = i * UNROLL + u
+                v = field[pl.ds(pl.multiple_of(k * BLOCK + which[0] * ROWS, 8), count * ROWS), :]
+                high = v.astype(BF16)
+                low = (v - high.astype(F32)).astype(BF16)
+                values.append(v)
+                sides.append(jnp.dot(jnp.concatenate([high, low], axis=1), shift, preferred_element_type=F32))
+            for u in range(UNROLL):
+                k = i * UNROLL + u
+                level = at_level(k, (c0, ce, cw, cn, cs, ca))
+                new = []
+                for n, t in enumerate(which):
+                    rows = slice(n * ROWS, (n + 1) * ROWS)
+                    new.append(stencil(
+                        k, t, level, carry[n], values[u][rows], sides[u][rows, :LANES], sides[u][rows, LANES:]
+                    ))
+                carry = tuple(new)
+            return carry
 
         zero = jnp.zeros((ROWS, LANES), F32)
-        last = lax.fori_loop(0, levels, down_body, (zero,) * TRACERS)
+        last = lax.fori_loop(0, levels // UNROLL, down_body, (zero,) * count)
 
         def up_body(i, carry):
             k = levels - 2 - i
             g = at_level(k, (cg,))[0]
             out = []
-            for t in range(TRACERS):
+            for t, below in zip(which, carry):
                 rows = pl.ds(pl.multiple_of(k * BLOCK + t * ROWS, 8), ROWS)
-                new = field[rows, :] + g * carry[t]
+                new = field[rows, :] + g * below
                 field[rows, :] = new
                 out.append(new)
             return tuple(out)
 
-        lax.fori_loop(0, levels - 1, up_body, last)
+        lax.fori_loop(0, levels - 1, up_body, last, unroll=4)
     else:
 
         def down_one(a, carry):
@@ -162,7 +198,7 @@
     adj_out, force_out, res_out,
     field, conc, we, wn, mix, prof, force, c0, ce, cw, cn, cs, ca, cg,
     kv, colv, obsv, errv, sendb, recvb, kn, coln, wres, resb,
-    lhs, rhs,
+    prof2, total,
     q_adj0, q_adj1, q_one, lat_a, lat_b, lat_one_a, lat_one_b,
     w_adj0, e_adj0, w_adj1, e_adj1, s_adj0, n_adj0, s_adj1, n_adj1,
     w_one, e_one, s_one, n_one, m_adj, m_one,
@@ -203,7 +239,7 @@
             pack_rows(kk, c, [kv[pl.ds(pl.multiple_of((kk * 4 + q) * tiles + c * 8, 8), 8), :] for q in range(4)])
         return carry
 
-    lax.fori_loop(0, levels // 4, pack_body, 0)
+    lax.fori_loop(0, levels // 4, pack_body, 0, unroll=3)
     for c in range(groups):
         rows = pl.ds(c * 8, 8)
         e = errv[rows, :]
@@ -253,20 +289,19 @@
         copy.start()
     halo = exchange(2, q_adj0, lat_a.at[0], lat_b.at[0], w_adj0, e_adj0, s_adj0, n_adj0)
 
-    def peer(i):
-        d = lax.rem(i * 37, bricks)
-        tl, ta = lax.rem(lon + d // n_lat, n_lon), lax.rem(lat + lax.rem(d, n_lat), n_lat)
-        return tl, ta, tl * n_lat + ta
-
-    def send_body(i, c):
-        tl, ta, t = peer(i)
+    lons = [lax.rem(lon + d, n_lon) for d in range(n_lon)]
+    lats = [lax.rem(lat + d, n_lat) for d in range(n_lat)]
+    peers = []
+    for i in range(1, bricks):
+        d = (i * 37) % bricks
+        tl, ta = lons[d // n_lat], lats[d % n_lat]
+        peers.append((tl, ta, tl * n_lat + ta))
+
+    for tl, ta, t in peers:
         pltpu.make_async_remote_copy(
             sendb.at[pl.ds(t * per, per)], recvb.at[pl.ds(me * per, per)], a2a_send, a2a_recv,
             device_id=(tl, ta), device_id_type=MESH,
         ).start()
-        return c
-
-    lax.fori_loop(1, bricks, send_body, 0)
     own = pltpu.make_async_copy(sendb.at[pl.ds(me * per, per)], recvb.at[pl.ds(me * per, per)], self_sem)
     own.start()
 
@@ -322,16 +357,11 @@
 
     land(halo)
     merge_lon(w_adj0, e_adj0, levels // 4, m_adj)
-    transport(field, levels, TRACERS, m_adj, s_adj0, n_adj0, coef)
+    transport(field, levels, range(TRACERS), m_adj, s_adj0, n_adj0, coef)
     pack_lon(field, levels, q_adj1)
     pack_lat(field, levels, ROWS - 1, lat_a.at[1])
     pack_lat(field, levels, 0, lat_b.at[1])
-    halo = exchange(6, q_adj1, lat_a.at[1], lat_b.at[1], w_adj1, e_adj1, s_adj1, n_adj1)
-    land(halo)
-    merge_lon(w_adj1, e_adj1, levels // 4, m_adj)
-    transport(field, levels, TRACERS, m_adj, s_adj1, n_adj1, coef)
-    adj_copy = pltpu.make_async_copy(field, adj_out, out_sem.at[0])
-    adj_copy.start()
+    adj_halo = exchange(6, q_adj1, lat_a.at[1], lat_b.at[1], w_adj1, e_adj1, s_adj1, n_adj1)
 
     own.wait()
     rest = pl.ds(0, (bricks - 1) * per)
@@ -348,91 +378,93 @@
                 kn[pl.ds(pl.multiple_of((kk * 4 + q) * tiles + c * 8, 8), 8), :] = v[q]
         return carry
 
-    lax.fori_loop(0, levels // 4, unpack_body, 0)
-    aux = [unpack(levels // 4, c) for c in range(groups)]
-    cols = [aux[c][0].astype(jnp.int32) for c in range(groups)]
-    spots = [lax.bitwise_and(v, LANES - 1) for v in cols]
-    bits = [[lax.bitwise_and(v, LANES << b) != 0 for b in range(4)] for v in cols]
-
-    def gather_body(k, acc):
-        rows = [
-            jnp.broadcast_to(prof[pl.ds(k * ROWS + r, 1), :], (8, LANES)) for r in range(ROWS)
-        ]
-        out = []
-        for c in range(groups):
-            picked = [jnp.take_along_axis(v, spots[c], axis=1, mode="promise_in_bounds") for v in rows]
-            for b in range(4):
-                picked = [jnp.where(bits[c][b], picked[2 * i + 1], picked[2 * i]) for i in range(len(picked) // 2)]
-            out.append(acc[c] + kn[pl.ds(pl.multiple_of(k * tiles + c * 8, 8), 8), :] * picked[0])
-        return tuple(out)
-
-    modelled = lax.fori_loop(0, levels, gather_body, (jnp.zeros((8, LANES), F32),) * groups)
+    lax.fori_loop(0, levels // 4, unpack_body, 0, unroll=3)
     for c in range(groups):
         rows = pl.ds(c * 8, 8)
-        res = jnp.where(cols[c] >= 0, (modelled[c] - aux[c][1]) / aux[c][2], 0.0)
-        wres[rows, :] = res
-        coln[rows, :] = cols[c]
-        obsv[rows, :] = res / aux[c][2]
-
-    def res_body(i, c):
-        tl, ta, t = peer(i)
+        aux = unpack(levels // 4, c)
+        coln[rows, :] = aux[0].astype(jnp.int32)
+        obsv[rows, :] = aux[1]
+        errv[rows, :] = aux[2]
+
+    for r in range(ROWS):
+        v = prof[pl.ds(r, levels, stride=ROWS), :]
+        high = v.astype(BF16)
+        rows, at = pl.ds(r // 2 * levels, levels), r % 2 * LANES
+        prof2[rows, pl.ds(at, LANES)] = high
+        prof2[rows, pl.ds(2 * LANES + at, LANES)] = (v - high.astype(F32)).astype(BF16)
+
+    cell = lax.broadcasted_iota(jnp.int32, (2 * LANES, 2 * LANES), 0)
+
+    def pair_of(ref, i):
+        return jnp.concatenate([ref[pl.ds(2 * i, 1), :], ref[pl.ds(2 * i + 1, 1), :]], axis=1)
+
+    def soundings(i, carry):
+        col, obs, err = pair_of(coln, i), pair_of(obsv, i), pair_of(errv, i)
+        half = lax.shift_right_arithmetic(col, 8)
+        hot = jnp.where(lax.bitwise_and(col, 2 * LANES - 1) == cell, 1.0, 0.0).astype(BF16)
+        g = jnp.dot(prof2[...], jnp.concatenate([hot, hot], axis=0), preferred_element_type=F32)
+        parts = [g[r * levels : (r + 1) * levels] for r in range(ROWS // 2)]
+        for b in range(3):
+            bit = lax.bitwise_and(half, 1 << b) != 0
+            parts = [jnp.where(bit, parts[2 * j + 1], parts[2 * j]) for j in range(len(parts) // 2)]
+        w = jnp.concatenate(
+            [kn[pl.ds(2 * i, levels, stride=tiles), :], kn[pl.ds(2 * i + 1, levels, stride=tiles), :]], axis=1
+        )
+        modelled = jnp.sum(w * parts[0], axis=0, keepdims=True)
+        res = jnp.where(col >= 0, (modelled - obs) / err, 0.0)
+        wres[pl.ds(2 * i, 1), :] = res[:, :LANES]
+        wres[pl.ds(2 * i + 1, 1), :] = res[:, LANES:]
+        w = w * (res / err)
+        high = w.astype(BF16).astype(F32)
+        low = w - high
+        lhs = jnp.concatenate(
+            [jnp.where(half == r, v, 0.0) for v in (high, low) for r in range(ROWS // 2)], axis=0
+        ).astype(BF16)
+        total[...] += lax.dot_general(lhs, hot, (((1,), (1,)), ((), ())), preferred_element_type=F32)
+        return carry
+
+    total[...] = jnp.zeros_like(total)
+    lax.fori_loop(0, tiles // 2, soundings, 0, unroll=4)
+
+    for r in range(ROWS):
+        lanes = pl.ds(r % 2 * LANES, LANES)
+        at = r // 2 * levels
+        force[pl.ds(r, levels, stride=ROWS), :] = (
+            total[pl.ds(at, levels), lanes] + total[pl.ds(levels * ROWS // 2 + at, levels), lanes]
+        )
+
+    def send_force(step):
+        pack_lon(force, levels // 8, q_one.at[step])
+        pack_lat(force, levels // 8, ROWS - 1, lat_one_a.at[step])
+        pack_lat(force, levels // 8, 0, lat_one_b.at[step])
+        return exchange(
+            6 + 4 * step, q_one.at[step], lat_one_a.at[step], lat_one_b.at[step],
+            w_one.at[step], e_one.at[step], s_one.at[step], n_one.at[step],
+        )
+
+    def step_force(step, halo):
+        land(halo)
+        merge_lon(w_one.at[step], e_one.at[step], (levels // 8 + 3) // 4, m_one)
+        transport(force, levels, None, m_one, s_one.at[step], n_one.at[step], coef)
+
+    halo = send_force(1)
+    land(adj_halo)
+    merge_lon(w_adj1, e_adj1, levels // 4, m_adj)
+    transport(field, levels, range(0, TRACERS // 2), m_adj, s_adj1, n_adj1, coef)
+    step_force(1, halo)
+    halo = send_force(2)
+    for tl, ta, t in peers:
         pltpu.make_async_remote_copy(
             wres.at[pl.ds(t // 4, 1)], resb.at[pl.ds(me, 1)], res_send, res_recv,
             device_id=(tl, ta), device_id_type=MESH,
         ).start()
-        return c
-
-    lax.fori_loop(1, bricks, res_body, 0)
     own_res = pltpu.make_async_copy(wres.at[pl.ds(me // 4, 1)], resb.at[pl.ds(me, 1)], self_sem)
     own_res.start()
 
-    def weigh(k, c):
-        for g in range(groups):
-            rows = pl.ds(pl.multiple_of(k * tiles + g * 8, 8), 8)
-            kn[rows, :] = kn[rows, :] * obsv[pl.ds(g * 8, 8), :]
-        return c
-
-    lax.fori_loop(0, levels, weigh, 0)
-
-    cell = lax.broadcasted_iota(jnp.int32, (2 * LANES, LANES), 0)
-
-    def build(c, carry):
-        lanes = pl.ds(pl.multiple_of(c * LANES, LANES), LANES)
-        w = kn[pl.ds(c, levels, stride=tiles), :]
-        high = w.astype(BF16)
-        low = (w - high.astype(F32)).astype(BF16)
-        lhs[pl.ds(0, levels), lanes] = high
-        lhs[pl.ds(levels, levels), lanes] = low
-        col = jnp.broadcast_to(coln[pl.ds(c, 1), :], (2 * LANES, LANES))
-        rhs[:, lanes] = jnp.where(lax.bitwise_and(col, 2 * LANES - 1) == cell, 1.0, 0.0).astype(BF16)
-        return carry
-
-    lax.fori_loop(0, tiles, build, 0)
-    colrow = jnp.concatenate([coln[pl.ds(c, 1), :] for c in range(tiles)], axis=1)
-
-    def scatter(r, carry):
-        mine = jnp.where(lax.shift_right_arithmetic(colrow, 8) == r, 1.0, 0.0).astype(BF16)
-        out = lax.dot_general(
-            lhs[...] * mine, rhs[...], (((1,), (1,)), ((), ())), preferred_element_type=F32
-        )
-        both = out[:levels] + out[levels:]
-        force[pl.ds(2 * r, levels, stride=ROWS), :] = both[:, :LANES]
-        force[pl.ds(2 * r + 1, levels, stride=ROWS), :] = both[:, LANES:]
-        return carry
-
-    lax.fori_loop(0, ROWS // 2, scatter, 0)
-
-    for step in (1, 2):
-        pack_lon(force, levels // 8, q_one.at[step])
-        pack_lat(force, levels // 8, ROWS - 1, lat_one_a.at[step])
-        pack_lat(force, levels // 8, 0, lat_one_b.at[step])
-        halo = exchange(
-            6 + 4 * step, q_one.at[step], lat_one_a.at[step], lat_one_b.at[step],
-            w_one.at[step], e_one.at[step], s_one.at[step], n_one.at[step],
-        )
-        land(halo)
-        merge_lon(w_one.at[step], e_one.at[step], (levels // 8 + 3) // 4, m_one)
-        transport(force, levels, 1, m_one, s_one.at[step], n_one.at[step], coef)
+    transport(field, levels, range(TRACERS // 2, TRACERS), m_adj, s_adj1, n_adj1, coef)
+    adj_copy = pltpu.make_async_copy(field, adj_out, out_sem.at[0])
+    adj_copy.start()
+    step_force(2, halo)
     force_copy = pltpu.make_async_copy(force, force_out, out_sem.at[1])
     force_copy.start()
 
@@ -441,12 +473,12 @@
     pltpu.make_async_copy(resb.at[rest_res], resb.at[rest_res], res_recv).wait()
     mine_block = lax.rem(me, 4)
     for g in range(groups):
-        total = jnp.zeros((8, LANES), F32)
+        mine = jnp.zeros((8, LANES), F32)
         for m in range(4):
             v = resb[pl.ds(g * 32 + m, 8, stride=4), :]
             shift = lax.rem((m - mine_block + 4) * 32, LANES)
-            total = jnp.where(lane8 // 32 == m, pltpu.roll(v, shift, 1), total)
-        errv[pl.ds(g * 8, 8), :] = total
+            mine = jnp.where(lane8 // 32 == m, pltpu.roll(v, shift, 1), mine)
+        errv[pl.ds(g * 8, 8), :] = mine
     res_copy = pltpu.make_async_copy(errv, res_out, out_sem.at[2])
     res_copy.start()
 
@@ -457,13 +489,40 @@
     res_copy.wait()
 
 
-def add_kernel(field, force, res, out, res_out):
-    for k in range(8):
-        one = force[k * ROWS : (k + 1) * ROWS, :]
-        for t in range(TRACERS):
-            rows = pl.ds(k * BLOCK + t * ROWS, ROWS)
-            out[rows, :] = field[rows, :] + one
-    res_out[...] = res[...]
+def add_kernel(levels, field, force, res, out, res_out, buf, one, rows_buf, in_sem, out_sem, aux_sem):
+    parts = levels // COMBINE
+    rows = COMBINE * BLOCK
+    aux = [
+        pltpu.make_async_copy(force, one, aux_sem.at[0]), pltpu.make_async_copy(res, rows_buf, aux_sem.at[1]),
+        pltpu.make_async_copy(rows_buf, res_out, aux_sem.at[2]),
+    ]
+    aux[0].start()
+    reads, writes = [], []
+    for p in range(parts):
+        at = pl.ds(p * rows, rows)
+        reads.append(pltpu.make_async_copy(field.at[at], buf.at[at], in_sem.at[p]))
+        writes.append(pltpu.make_async_copy(buf.at[at], out.at[at], out_sem.at[p]))
+        reads[p].start()
+    aux[1].start()
+    aux[0].wait()
+    for p in range(parts):
+        reads[p].wait()
+
+        def body(k, c):
+            add = one[pl.ds(pl.multiple_of(k * ROWS, ROWS), ROWS), :]
+            for t in range(TRACERS):
+                at = pl.ds(pl.multiple_of(k * BLOCK + t * ROWS, ROWS), ROWS)
+                buf[at, :] = buf[at, :] + add
+            return c
+
+        lax.fori_loop(p * COMBINE, (p + 1) * COMBINE, body, 0, unroll=4)
+        writes[p].start()
+        if p == 0:
+            aux[1].wait()
+            aux[2].start()
+    for copy in writes:
+        copy.wait()
+    aux[2].wait()
 
 
 def per_device(n_lon, n_lat, concentration, adjoint, wind_east, wind_north, mixing, sound_col, kernel, observed, obs_error):
@@ -481,7 +540,7 @@
         + [vm(levels * tiles, LANES), pltpu.VMEM((tiles, LANES), jnp.int32), vm(tiles, LANES), vm(tiles, LANES)]
         + [vm(bricks * per, LANES), vm(bricks * per, LANES), vm(levels * tiles, LANES)]
         + [pltpu.VMEM((tiles, LANES), jnp.int32), vm(tiles, LANES), vm(bricks, LANES)]
-        + [pltpu.VMEM((2 * levels, slots), BF16), pltpu.VMEM((2 * LANES, slots), BF16)]
+        + [pltpu.VMEM((ROWS // 2 * levels, 4 * LANES), BF16), vm(ROWS * levels, 2 * LANES)]
         + [vm(q_rows, LANES), vm(q_rows, LANES), vm(3, q_one_rows, LANES)]
         + [vm(2, levels * 8, LANES), vm(2, levels * 8, LANES), vm(3, levels, LANES), vm(3, levels, LANES)]
         + [vm(q_rows, LANES)] * 4 + [vm(levels * 8, LANES)] * 4
@@ -499,23 +558,24 @@
         in_specs=[hbm] * 9,
         out_specs=(hbm,) * 3,
         scratch_shapes=scratch,
-        compiler_params=pltpu.CompilerParams(collective_id=0, has_side_effects=True, vmem_limit_bytes=48 << 20),
+        compiler_params=pltpu.CompilerParams(collective_id=0, has_side_effects=True, vmem_limit_bytes=62 << 20),
         name="window",
     )(
         concentration.reshape(big), adjoint.reshape(big), wind_east.reshape(one), wind_north.reshape(one),
         mixing.reshape(one), sound_col.reshape(tiles, LANES), kernel.reshape(levels * tiles, LANES),
         observed.reshape(tiles, LANES), obs_error.reshape(tiles, LANES),
     )
+    parts = levels // COMBINE
     out, residual = pl.pallas_call(
-        add_kernel,
-        grid=(levels // 8,),
+        functools.partial(add_kernel, levels),
         out_shape=(jax.ShapeDtypeStruct(big, F32), jax.ShapeDtypeStruct((tiles, LANES), F32)),
-        in_specs=[
-            pl.BlockSpec((8 * BLOCK, LANES), lambda i: (i, 0)),
-            pl.BlockSpec((8 * ROWS, LANES), lambda i: (i, 0)),
-            pl.BlockSpec((tiles, LANES), lambda i: (0, 0)),
+        in_specs=[hbm] * 3,
+        out_specs=(hbm, hbm),
+        scratch_shapes=[
+            vm(*big), vm(*one), vm(tiles, LANES),
+            pltpu.SemaphoreType.DMA((parts,)), pltpu.SemaphoreType.DMA((parts,)), pltpu.SemaphoreType.DMA((3,)),
         ],
-        out_specs=(pl.BlockSpec((8 * BLOCK, LANES), lambda i: (i, 0)), pl.BlockSpec((tiles, LANES), lambda i: (0, 0))),
+        compiler_params=pltpu.CompilerParams(vmem_limit_bytes=62 << 20),
         name="combine",
     )(field, force, res)
     return out.reshape(adjoint.shape), residual.reshape(observed.shape)

time: 119 us -> 70.6 us (0.59)
  Pallas kernels: 109 us -> 69.8 us
  local copies, waits for them, and re-layouts: 8.02 us -> 0 us
    pallas_call x1, Pallas kernels: 102 us -> 65.2 us  [per_device(): pl.pallas_call(functools.partial(window_kernel, n_lon, n_lat, levels), ou...]
    unnamed x18 -> x0, local copies, waits for them, and re-layouts: 8.02 us -> none
    pallas_call x1, Pallas kernels: 7.4 us -> 4.57 us  [per_device(): pl.pallas_call(functools.partial(add_kernel, levels), out_shape=(jax.Shap...]
where the time goes in v1:
time: 70.6 us; the launch traced here: 70.5 us
  Pallas kernels  69.8 us (99%)
    pallas_call x1, Pallas kernels, per_device(): pl.pallas_call(functools.partial(window_kernel, n_lon, n_lat, levels), ou...  65.2 us
    pallas_call x1, Pallas kernels, per_device(): pl.pallas_call(functools.partial(add_kernel, levels), out_shape=(jax.Shap...  4.57 us

profile of v1, /device:TPU:1, one launch (start us, length us, event | category | flops | bytes accessed | tf_op | source)
XLA Modules:
  0.0 70.5 jit_solution(10683308797433578922)
XLA Ops:
  0.6 65.2 %window.1 = (f32[9216,128]{1,0:T(8,128)}, f32[1152,128]{1,0:T(8,128)}, f32[32,128]{1,0:T(8,128)}) custom-call(f32[9216,128]{1,0:T(8,128)} %bitcast.11, f32[9216,128]{1,0:T(8,128)} %bitcast.12, f32[1152,128]{1,0:T(8,128)} %bitcast.14, f32[1152,128]{1,0:T(8,128)} %bitcast.15, f32[1152,128]{1,0:T(8,128)} %bitcast.16, s32[32,128]{1,0:T(8,128)} %bitcast.17, ...), custom_call_target="tpu_custom_call" | custom-call | tf_op jit(solution)/shard_map/window/pallas_call | solution.py:553
  65.9 4.6 %combine.1 = (f32[9216,128]{1,0:T(8,128)}, f32[32,128]{1,0:T(8,128)}) custom-call(f32[9216,128]{1,0:T(8,128)} %get-tuple-element.7.field, f32[1152,128]{1,0:T(8,128)} %get-tuple-element.8.force, f32[32,128]{1,0:T(8,128)} %get-tuple-element.9.res), custom_call_target="tpu_custom_call" | custom-call | tf_op jit(solution)/shard_map/combine/pallas_call | solution.py:569

commit v2 on v1

--- a/solution.py
+++ b/solution.py
@@ -66,7 +66,7 @@
         group(g, 4)
         return c
 
-    lax.fori_loop(0, blocks // 4, body, 0)
+    lax.fori_loop(0, blocks // 4, body, 0, unroll=3)
     if blocks % 4:
         group(blocks // 4, blocks % 4)
 
@@ -226,38 +226,44 @@
         pl.semaphore_signal(barrier, inc=1, device_id=(lax.rem(lon + d, n_lon), lat), device_id_type=MESH)
 
     lane8 = lane_ids(8)
-    for i in range(4):
-        loads[i].wait()
-
-    def pack_rows(kk, c, v):
-        y = swap_blocks(v, lane8)
-        for m in range(4):
-            sendb[pl.ds((c * 32 + m) * per + kk, 8, stride=4 * per), :] = y[m]
-
-    def pack_body(kk, carry):
+
+    def pack_soundings():
+        for i in range(4):
+            loads[i].wait()
+
+        def pack_rows(kk, c, v):
+            y = swap_blocks(v, lane8)
+            for m in range(4):
+                sendb[pl.ds((c * 32 + m) * per + kk, 8, stride=4 * per), :] = y[m]
+
+        def pack_body(kk, carry):
+            for c in range(groups):
+                pack_rows(kk, c, [kv[pl.ds(pl.multiple_of((kk * 4 + q) * tiles + c * 8, 8), 8), :] for q in range(4)])
+            return carry
+
+        lax.fori_loop(0, levels // 4, pack_body, 0, unroll=3)
         for c in range(groups):
-            pack_rows(kk, c, [kv[pl.ds(pl.multiple_of((kk * 4 + q) * tiles + c * 8, 8), 8), :] for q in range(4)])
-        return carry
-
-    lax.fori_loop(0, levels // 4, pack_body, 0, unroll=3)
-    for c in range(groups):
-        rows = pl.ds(c * 8, 8)
-        e = errv[rows, :]
-        pack_rows(levels // 4, c, [colv[rows, :].astype(F32), obsv[rows, :], e, e])
-
-    loads[4].wait()
-    loads[5].wait()
-    pack_lon(we, levels // 8, q_one.at[0])
-    pack_lat(wn, levels // 8, ROWS - 1, lat_one_a.at[0])
-    loads[6].wait()
-    pack_lon(field, levels, q_adj0)
-    pack_lat(field, levels, ROWS - 1, lat_a.at[0])
-    pack_lat(field, levels, 0, lat_b.at[0])
-
-    pl.semaphore_wait(barrier, n_lon + n_lat - 2)
-    for d in range(1, n_lat):
-        pl.semaphore_signal(stage_sem, inc=1, device_id=(lon, lax.rem(lat + d, n_lat)), device_id_type=MESH)
-    pl.semaphore_wait(stage_sem, n_lat - 1)
+            rows = pl.ds(c * 8, 8)
+            e = errv[rows, :]
+            pack_rows(levels // 4, c, [colv[rows, :].astype(F32), obsv[rows, :], e, e])
+
+
+    def pack_halos():
+        loads[4].wait()
+        loads[5].wait()
+        pack_lon(we, levels // 8, q_one.at[0])
+        pack_lat(wn, levels // 8, ROWS - 1, lat_one_a.at[0])
+        loads[6].wait()
+        pack_lon(field, levels, q_adj0)
+        pack_lat(field, levels, ROWS - 1, lat_a.at[0])
+        pack_lat(field, levels, 0, lat_b.at[0])
+
+
+    def enter():
+        pl.semaphore_wait(barrier, n_lon + n_lat - 2)
+        for d in range(1, n_lat):
+            pl.semaphore_signal(stage_sem, inc=1, device_id=(lon, lax.rem(lat + d, n_lat)), device_id_type=MESH)
+        pl.semaphore_wait(stage_sem, n_lat - 1)
 
     east = (lax.rem(lon + 1, n_lon), lat)
     west = (lax.rem(lon + n_lon - 1, n_lon), lat)
@@ -282,12 +288,14 @@
         for copy in copies:
             copy.wait()
 
-    wind_copies = [
-        remote(q_one.at[0], w_one.at[0], 0, east), remote(lat_one_a.at[0], s_one.at[0], 1, north),
-    ]
-    for copy in wind_copies:
-        copy.start()
-    halo = exchange(2, q_adj0, lat_a.at[0], lat_b.at[0], w_adj0, e_adj0, s_adj0, n_adj0)
+    def send_halos():
+        wind_copies = [
+            remote(q_one.at[0], w_one.at[0], 0, east), remote(lat_one_a.at[0], s_one.at[0], 1, north),
+        ]
+        for copy in wind_copies:
+            copy.start()
+        halo = exchange(2, q_adj0, lat_a.at[0], lat_b.at[0], w_adj0, e_adj0, s_adj0, n_adj0)
+        return wind_copies, halo
 
     lons = [lax.rem(lon + d, n_lon) for d in range(n_lon)]
     lats = [lax.rem(lat + d, n_lat) for d in range(n_lat)]
@@ -297,25 +305,35 @@
         tl, ta = lons[d // n_lat], lats[d % n_lat]
         peers.append((tl, ta, tl * n_lat + ta))
 
-    for tl, ta, t in peers:
-        pltpu.make_async_remote_copy(
-            sendb.at[pl.ds(t * per, per)], recvb.at[pl.ds(me * per, per)], a2a_send, a2a_recv,
-            device_id=(tl, ta), device_id_type=MESH,
-        ).start()
+    def send_soundings(which):
+        for tl, ta, t in which:
+            pltpu.make_async_remote_copy(
+                sendb.at[pl.ds(t * per, per)], recvb.at[pl.ds(me * per, per)], a2a_send, a2a_recv,
+                device_id=(tl, ta), device_id_type=MESH,
+            ).start()
+
+    def sum_tracers():
+        loads[8].wait()
+
+        def tracer_sum(k, c):
+            total = conc[pl.ds(pl.multiple_of(k * BLOCK, 8), ROWS), :]
+            for t in range(1, TRACERS):
+                total = total + conc[pl.ds(pl.multiple_of(k * BLOCK + t * ROWS, 8), ROWS), :]
+            prof[pl.ds(pl.multiple_of(k * ROWS, 8), ROWS), :] = total
+            return c
+
+        lax.fori_loop(0, levels, tracer_sum, 0, unroll=2)
+
     own = pltpu.make_async_copy(sendb.at[pl.ds(me * per, per)], recvb.at[pl.ds(me * per, per)], self_sem)
+    pack_soundings()
+    enter()
+    send_soundings(peers[: bricks // 2])
+    pack_halos()
+    wind_copies, halo = send_halos()
+    send_soundings(peers[bricks // 2 :])
     own.start()
-
+    sum_tracers()
     loads[7].wait()
-    loads[8].wait()
-
-    def tracer_sum(k, c):
-        total = conc[pl.ds(pl.multiple_of(k * BLOCK, 8), ROWS), :]
-        for t in range(1, TRACERS):
-            total = total + conc[pl.ds(pl.multiple_of(k * BLOCK + t * ROWS, 8), ROWS), :]
-        prof[pl.ds(pl.multiple_of(k * ROWS, 8), ROWS), :] = total
-        return c
-
-    lax.fori_loop(0, levels, tracer_sum, 0, unroll=2)
 
     land(wind_copies)
     lane = lane_ids(ROWS)

time: 70.6 us -> 67.4 us (0.955)
  Pallas kernels: 69.8 us -> 66.7 us
    pallas_call x1, Pallas kernels: 65.2 us -> 62.1 us  [per_device(): pl.pallas_call(functools.partial(window_kernel, n_lon, n_lat, levels), ou...]
where the time goes in v2:
time: 67.4 us; the launch traced here: 67.3 us
  Pallas kernels  66.7 us (99%)
    pallas_call x1, Pallas kernels, per_device(): pl.pallas_call(functools.partial(window_kernel, n_lon, n_lat, levels), ou...  62.1 us
    pallas_call x1, Pallas kernels, per_device(): pl.pallas_call(functools.partial(add_kernel, levels), out_shape=(jax.Shap...  4.57 us

profile of v2, /device:TPU:1, one launch (start us, length us, event | category | flops | bytes accessed | tf_op | source)
XLA Modules:
  0.0 67.3 jit_solution(15409363287730598348)
XLA Ops:
  0.6 62.1 %window.1 = (f32[9216,128]{1,0:T(8,128)}, f32[1152,128]{1,0:T(8,128)}, f32[32,128]{1,0:T(8,128)}) custom-call(f32[9216,128]{1,0:T(8,128)} %bitcast.11, f32[9216,128]{1,0:T(8,128)} %bitcast.12, f32[1152,128]{1,0:T(8,128)} %bitcast.14, f32[1152,128]{1,0:T(8,128)} %bitcast.15, f32[1152,128]{1,0:T(8,128)} %bitcast.16, s32[32,128]{1,0:T(8,128)} %bitcast.17, ...), custom_call_target="tpu_custom_call" | custom-call | tf_op jit(solution)/shard_map/window/pallas_call | solution.py:571
  62.7 4.6 %combine.1 = (f32[9216,128]{1,0:T(8,128)}, f32[32,128]{1,0:T(8,128)}) custom-call(f32[9216,128]{1,0:T(8,128)} %get-tuple-element.7.field, f32[1152,128]{1,0:T(8,128)} %get-tuple-element.8.force, f32[32,128]{1,0:T(8,128)} %get-tuple-element.9.res), custom_call_target="tpu_custom_call" | custom-call | tf_op jit(solution)/shard_map/combine/pallas_call | solution.py:587

commit v3 on v2

--- a/solution.py
+++ b/solution.py
@@ -325,13 +325,12 @@
         lax.fori_loop(0, levels, tracer_sum, 0, unroll=2)
 
     own = pltpu.make_async_copy(sendb.at[pl.ds(me * per, per)], recvb.at[pl.ds(me * per, per)], self_sem)
+    early = bricks * 3 // 8
     pack_soundings()
     enter()
-    send_soundings(peers[: bricks // 2])
+    send_soundings(peers[:early])
     pack_halos()
     wind_copies, halo = send_halos()
-    send_soundings(peers[bricks // 2 :])
-    own.start()
     sum_tracers()
     loads[7].wait()
 
@@ -374,6 +373,8 @@
     coef = (c0, ce, cw, cn, cs, ca, cg)
 
     land(halo)
+    send_soundings(peers[early:])
+    own.start()
     merge_lon(w_adj0, e_adj0, levels // 4, m_adj)
     transport(field, levels, range(TRACERS), m_adj, s_adj0, n_adj0, coef)
     pack_lon(field, levels, q_adj1)

time: 67.4 us -> 63.4 us (0.941)
  Pallas kernels: 66.7 us -> 62.6 us
    pallas_call x1, Pallas kernels: 62.1 us -> 58.1 us  [per_device(): pl.pallas_call(functools.partial(window_kernel, n_lon, n_lat, levels), ou...]
where the time goes in v3:
time: 63.4 us; the launch traced here: 63.3 us
  Pallas kernels  62.6 us (99%)
  between operations  0.64 us (1%)
    pallas_call x1, Pallas kernels, per_device(): pl.pallas_call(functools.partial(window_kernel, n_lon, n_lat, levels), ou...  58.1 us
    pallas_call x1, Pallas kernels, per_device(): pl.pallas_call(functools.partial(add_kernel, levels), out_shape=(jax.Shap...  4.57 us

profile of v3, /device:TPU:1, one launch (start us, length us, event | category | flops | bytes accessed | tf_op | source)
XLA Modules:
  0.0 63.3 jit_solution(12626328877999951947)
XLA Ops:
  0.6 58.1 %window.1 = (f32[9216,128]{1,0:T(8,128)}, f32[1152,128]{1,0:T(8,128)}, f32[32,128]{1,0:T(8,128)}) custom-call(f32[9216,128]{1,0:T(8,128)} %bitcast.11, f32[9216,128]{1,0:T(8,128)} %bitcast.12, f32[1152,128]{1,0:T(8,128)} %bitcast.14, f32[1152,128]{1,0:T(8,128)} %bitcast.15, f32[1152,128]{1,0:T(8,128)} %bitcast.16, s32[32,128]{1,0:T(8,128)} %bitcast.17, ...), custom_call_target="tpu_custom_call" | custom-call | tf_op jit(solution)/shard_map/window/pallas_call | solution.py:572
  58.7 4.6 %combine.1 = (f32[9216,128]{1,0:T(8,128)}, f32[32,128]{1,0:T(8,128)}) custom-call(f32[9216,128]{1,0:T(8,128)} %get-tuple-element.7.field, f32[1152,128]{1,0:T(8,128)} %get-tuple-element.8.force, f32[32,128]{1,0:T(8,128)} %get-tuple-element.9.res), custom_call_target="tpu_custom_call" | custom-call | tf_op jit(solution)/shard_map/combine/pallas_call | solution.py:588
